TPU v7x, 32 devices: a whole 2x2x4 slice. The times are simulated.
32 devices in a mesh: fsdp: 8 (over y, x, core), ep: 4 (over z).
Axes of the slice: x: 2, y: 2, z: 4, core: 2. Of those that a mesh axis runs over, the one named last changes fastest.
Arguments:
- hidden: bfloat16 [2048, 8192], P('fsdp', 'ep'), may hold values from -6 to 6
- w_down: bfloat16 [6144, 2, 8192], P('fsdp', None, 'ep'), may hold values from -0.0625 to 0.0625
- route_ids: int32 [1024, 2], P('fsdp'), may hold values from 0 to 7, as said below
- probs: float32 [1024, 2], P('fsdp'), may hold values from 0.1 to 0.9
- grad_out: bfloat16 [1024, 6144], P('fsdp', 'ep'), may hold values from -6 to 6
Outputs:
- output: bfloat16 [1024, 6144], P('fsdp', 'ep')
- grad_hidden: bfloat16 [2048, 8192], P('fsdp', 'ep')
- grad_weight: bfloat16 [6144, 2, 8192], P('fsdp', None, 'ep')
- grad_probs: float32 [1024, 2], P('fsdp')
Inputs may be any that keep to these rules, and one draw needn't show every extreme that they name: `route_ids`: each token names 2 different experts. Within one panel's 128 tokens, experts 0 and 1 are each named by 1 to 128 tokens, and in some panel both are named by all 128 tokens.
All inputs are finite; a program needn't handle non-finite values.
Results may differ from a plain program's by a relative error of at most 0.012.
Values may be sent and summed in bfloat16 or wider, within the bound.
A program may use at most 384 MiB of HBM per device.

v0:
```python
import jax
import jax.numpy as jnp
from jax import lax
from jax.sharding import PartitionSpec as P

BLOCK = 128


def route_layout(route_part, prob_part, expert_count, block_rows, row_count):
    token_count = route_part.shape[0]
    experts = jnp.arange(expert_count, dtype=jnp.int32)
    hits = (route_part[:, :, None] == experts[None, None, :]).astype(jnp.int32)
    named = jnp.sum(hits, axis=1)
    counts = jnp.sum(named, axis=0)
    ranks = jnp.cumsum(named, axis=0) - named
    padded = (counts + block_rows - 1) // block_rows * block_rows
    offsets = jnp.cumsum(padded) - padded
    row_of = jnp.sum(hits * (offsets[None, None, :] + ranks[:, None, :]), axis=2)
    valid = jnp.sum(hits, axis=2)
    starts = jnp.arange(row_count // block_rows, dtype=jnp.int32) * block_rows
    inside = (starts[:, None] >= offsets[None, :]) & (starts[:, None] < (offsets + padded)[None, :])
    block_exp = jnp.sum(jnp.where(inside, experts[None, :] + 1, 0), axis=1) - 1
    target = jnp.where(valid > 0, row_of, row_count).reshape(-1)
    token_index = jnp.broadcast_to(
        jnp.arange(token_count, dtype=jnp.int32)[:, None], route_part.shape
    ).reshape(-1)
    row_tok = jnp.zeros((row_count,), jnp.int32).at[target].set(token_index, mode="drop")
    row_live = (
        jnp.zeros((row_count,), jnp.int32).at[target].set(jnp.ones_like(token_index), mode="drop")
    )
    row_prob = (
        jnp.zeros((row_count,), prob_part.dtype).at[target].set(prob_part.reshape(-1), mode="drop")
    )
    return (row_of, valid, block_exp, row_tok, row_live, row_prob)


def local(hidden, w_down, route_ids, probs, grad_out):
    row_count, unit_count = hidden.shape
    expert_count = w_down.shape[1]
    block_count = row_count // BLOCK
    row_of, valid, block_exp, row_tok, row_live, row_prob = route_layout(
        route_ids, probs, expert_count, BLOCK, row_count
    )
    safe_exp = jnp.maximum(block_exp, 0)
    prob_valid = probs * valid.astype(jnp.float32)
    full_grads = lax.all_gather(grad_out, "ep", axis=1, tiled=True)
    model_width = full_grads.shape[1]
    routed = jnp.where(row_live[:, None] > 0, full_grads[row_tok], jnp.zeros((), jnp.bfloat16))
    scaled = (row_prob[:, None] * routed.astype(jnp.float32)).astype(jnp.bfloat16)
    hid_blocks = hidden.reshape(block_count, BLOCK, unit_count)
    routed_blocks = routed.reshape(block_count, BLOCK, model_width)
    row_exp = jnp.repeat(block_exp, BLOCK)
    member = (row_exp[:, None] == jnp.arange(expert_count, dtype=jnp.int32)[None, :]).astype(
        jnp.bfloat16
    )
    masked_hid = hidden[:, None, :] * member[:, :, None]
    piece = lax.all_gather(w_down, "fsdp", axis=0, tiled=True)
    width = piece.shape[0]
    chosen = jnp.take(piece, safe_exp, axis=1)
    out_rows = jnp.einsum(
        "bri,dbi->brd", hid_blocks, chosen, preferred_element_type=jnp.float32
    ).reshape(row_count, width)
    back_total = jnp.einsum(
        "brd,dbi->bri", routed_blocks, chosen, preferred_element_type=jnp.float32
    )
    combined = jnp.sum(prob_valid[:, :, None] * out_rows[row_of], axis=1)
    out_total = combined
    out_total, back_total = (out_total, back_total)
    grad_weight = lax.psum_scatter(
        jnp.einsum("rd,rei->dei", scaled, masked_hid, preferred_element_type=jnp.float32).astype(
            jnp.bfloat16
        ),
        "fsdp",
        scatter_dimension=0,
        tiled=True,
    )
    output = lax.psum_scatter(out_total.astype(jnp.bfloat16), "ep", scatter_dimension=1, tiled=True)
    hidden_back = back_total.reshape(row_count, unit_count)
    grad_hidden = (row_prob[:, None] * hidden_back).astype(jnp.bfloat16)
    row_dot = jnp.sum(hidden.astype(jnp.float32) * hidden_back, axis=1)
    prob_terms = valid.astype(jnp.float32) * row_dot[row_of]
    grad_probs = lax.psum(prob_terms, "ep")
    return (output, grad_hidden, grad_weight, grad_probs)


def solution(mesh):
    placed = (
        P("fsdp", "ep"),
        P("fsdp", None, "ep"),
        P("fsdp", None),
        P("fsdp", None),
        P("fsdp", "ep"),
    )
    return jax.shard_map(
        local,
        mesh=mesh,
        in_specs=placed,
        out_specs=(P("fsdp", "ep"), P("fsdp", "ep"), P("fsdp", None, "ep"), P("fsdp", None)),
        check_vma=False,
    )
```

profile of v0, /device:TPU:0, one launch (start us, length us, event | category | flops | bytes accessed | tf_op | source)
XLA Modules:
  0.0 635.5 jit_solution(14992355778642910269)
XLA Ops:
  7.9 8.4 %copy.21 = bf16[768,2,2048]{2,0,1:T(8,128)(2,1)} copy(bf16[768,2,2048]{2,1,0:T(2,128)(2,1)} %param.6) | data formatting | bytes 12582912 | tf_op args[1]
  23.5 25.9 %all-gather.5.cloned.1.call-done = bf16[128,6144]{1,0:T(8,128)(2,1)} async-done(((bf16[128,1536]{1,0:T(8,128)(2,1)}), bf16[128,6144]{1,0:T(8,128)(2,1)}) %all-gather.5.cloned.1.call-update) | async-done | bytes 1572880 | tf_op jit(solution)/shard_map/all_gather | solution.py:46
  49.4 7.1 %gather_fusion.1 = bf16[256,6144]{1,0:T(8,128)(2,1)S(1)} fusion(bf16[128,6144]{1,0:T(8,128)(2,1)} %all-gather.5.cloned.1.call-done, s32[1024]{0:T(1024)S(1)} %pad_clamp_fusion), kind=kCustom, calls=%fused_computation.1 | custom fusion | bytes 6292480 | tf_op jit(solution)/shard_map/gather | solution.py:48
  56.5 24.9 %convolution_convert_fusion = bf16[6144,2,2048]{2,0,1:T(8,128)(2,1)} fusion(bf16[256,6144]{1,0:T(8,128)(2,1)S(1)} %gather_fusion.1, f32[256]{0:T(256)S(1)} %scatter_custom_fusion, pred[256]{0:T(512)(128)(4,1)S(1)} %broadcast_compare_fusion, bf16[256,2]{0,1:T(2,128)(2,1)S(1)} %compare_convert_fusion, bf16[256,2048]{1,0:T(8,128)(2,1)} %param.5), kind=kOutput, calls=%fused_computation.31 | convolution fusion | flops 12920553472 | bytes 54528256 | tf_op jit(solution)/shard_map/rd,rei->dei/dot_general | solution.py:70
  83.2 199.5 %all-gather.3.cloned.1.call-done = bf16[6144,2,2048]{2,0,1:T(8,128)(2,1)} async-done(((bf16[768,2,2048]{2,0,1:T(8,128)(2,1)}), bf16[6144,2,2048]{2,0,1:T(8,128)(2,1)}) %all-gather.3.cloned.1.call-update) | async-done | bytes 50331664 | tf_op jit(solution)/shard_map/all_gather | solution.py:57
  282.7 41.5 %fusion.28 = (bf16[512,2,2048]{2,0,1:T(8,128)(2,1)}, bf16[512,2,2048]{2,0,1:T(8,128)(2,1)}, bf16[512,2,2048]{2,0,1:T(8,128)(2,1)}, bf16[512,2,2048]{2,0,1:T(8,12...) fusion(bf16[6144,2,2048]{2,0,1:T(8,128)(2,1)} %all-gather.3.clo, ...), kind=kLoop, calls=%fused_computation.108 | loop fusion | bytes 100663296 | tf_op jit(solution)/shard_map/jit(_take)/gather | solution.py:59
  327.2 9.6 %while.12 = (s32[]{:T(128)}, bf16[512,2,2048]{2,0,1:T(8,128)(2,1)}, s32[2,1]{0,1:T(1,128)S(1)}, bf16[2,512,2048]{2,1,0:T(8,128)(2,1)}, s32[]{:T(128)}) while((s32[]{:T(128)}, bf16[512,2,2048]{2,0,1:T(8,128)(2,1)}, s32[2,1]{0,1:T(1,128)S(1)}, bf16[2,512,2048]{2,1,0:T(8,128)(2,1)}, s32[]{:T(128)}) %tuple.161), condition=%wide.while_cond, body=%wide.while_body.sunk | while | flops 2 | bytes 4195401 | solution.py:59
  327.8 4.2 bitcast_dynamic-update-slice_fusion.36
  332.5 4.3 bitcast_dynamic-update-slice_fusion.36
  339.9 9.5 %while.13 = (s32[]{:T(128)}, bf16[512,2,2048]{2,0,1:T(8,128)(2,1)}, s32[2,1]{0,1:T(1,128)S(1)}, bf16[2,512,2048]{2,1,0:T(8,128)(2,1)}, s32[]{:T(128)}) while((s32[]{:T(128)}, bf16[512,2,2048]{2,0,1:T(8,128)(2,1)}, s32[2,1]{0,1:T(1,128)S(1)}, bf16[2,512,2048]{2,1,0:T(8,128)(2,1)}, s32[]{:T(128)}) %tuple.205), condition=%wide.while_cond.1, body=%wide.while_body.1.sunk | while | flops 2 | bytes 4195401 | solution.py:59
  340.5 4.3 bitcast_dynamic-update-slice_fusion.37
  352.0 8.8 %while.14 = (s32[]{:T(128)}, bf16[512,2,2048]{2,0,1:T(8,128)(2,1)}, s32[2,1]{0,1:T(1,128)S(1)}, bf16[2,512,2048]{2,1,0:T(8,128)(2,1)}, s32[]{:T(128)}) while((s32[]{:T(128)}, bf16[512,2,2048]{2,0,1:T(8,128)(2,1)}, s32[2,1]{0,1:T(1,128)S(1)}, bf16[2,512,2048]{2,1,0:T(8,128)(2,1)}, s32[]{:T(128)}) %tuple.206), condition=%wide.while_cond.2, body=%wide.while_body.2.sunk | while | flops 2 | bytes 4195401 | solution.py:59
  363.4 9.2 %while.15 = (s32[]{:T(128)}, bf16[512,2,2048]{2,0,1:T(8,128)(2,1)}, s32[2,1]{0,1:T(1,128)S(1)}, bf16[2,512,2048]{2,1,0:T(8,128)(2,1)}, s32[]{:T(128)}) while((s32[]{:T(128)}, bf16[512,2,2048]{2,0,1:T(8,128)(2,1)}, s32[2,1]{0,1:T(1,128)S(1)}, bf16[2,512,2048]{2,1,0:T(8,128)(2,1)}, s32[]{:T(128)}) %tuple.207), condition=%wide.while_cond.3, body=%wide.while_body.3.sunk | while | flops 2 | bytes 4195401 | solution.py:59
  375.1 9.1 %while.16 = (s32[]{:T(128)}, bf16[512,2,2048]{2,0,1:T(8,128)(2,1)}, s32[2,1]{0,1:T(1,128)S(1)}, bf16[2,512,2048]{2,1,0:T(8,128)(2,1)}, s32[]{:T(128)}) while((s32[]{:T(128)}, bf16[512,2,2048]{2,0,1:T(8,128)(2,1)}, s32[2,1]{0,1:T(1,128)S(1)}, bf16[2,512,2048]{2,1,0:T(8,128)(2,1)}, s32[]{:T(128)}) %tuple.208), condition=%wide.while_cond.4, body=%wide.while_body.4.sunk | while | flops 2 | bytes 4195401 | solution.py:59
  386.7 8.8 %while.17 = (s32[]{:T(128)}, bf16[512,2,2048]{2,0,1:T(8,128)(2,1)}, s32[2,1]{0,1:T(1,128)S(1)}, bf16[2,512,2048]{2,1,0:T(8,128)(2,1)}, s32[]{:T(128)}) while((s32[]{:T(128)}, bf16[512,2,2048]{2,0,1:T(8,128)(2,1)}, s32[2,1]{0,1:T(1,128)S(1)}, bf16[2,512,2048]{2,1,0:T(8,128)(2,1)}, s32[]{:T(128)}) %tuple.209), condition=%wide.while_cond.5, body=%wide.while_body.5.sunk | while | flops 2 | bytes 4195401 | solution.py:59
  398.1 8.8 %while.18 = (s32[]{:T(128)}, bf16[512,2,2048]{2,0,1:T(8,128)(2,1)}, s32[2,1]{0,1:T(1,128)S(1)}, bf16[2,512,2048]{2,1,0:T(8,128)(2,1)}, s32[]{:T(128)}) while((s32[]{:T(128)}, bf16[512,2,2048]{2,0,1:T(8,128)(2,1)}, s32[2,1]{0,1:T(1,128)S(1)}, bf16[2,512,2048]{2,1,0:T(8,128)(2,1)}, s32[]{:T(128)}) %tuple.210), condition=%wide.while_cond.6, body=%wide.while_body.6.sunk | while | flops 2 | bytes 4195401 | solution.py:59
  409.4 9.3 %while.19 = (s32[]{:T(128)}, bf16[512,2,2048]{2,0,1:T(8,128)(2,1)}, s32[2,1]{0,1:T(1,128)S(1)}, bf16[2,512,2048]{2,1,0:T(8,128)(2,1)}, s32[]{:T(128)}) while((s32[]{:T(128)}, bf16[512,2,2048]{2,0,1:T(8,128)(2,1)}, s32[2,1]{0,1:T(1,128)S(1)}, bf16[2,512,2048]{2,1,0:T(8,128)(2,1)}, s32[]{:T(128)}) %tuple.211), condition=%wide.while_cond.7, body=%wide.while_body.7.sunk | while | flops 2 | bytes 4195401 | solution.py:59
  410.0 4.2 bitcast_dynamic-update-slice_fusion.43
  421.2 8.8 %while.20 = (s32[]{:T(128)}, bf16[512,2,2048]{2,0,1:T(8,128)(2,1)}, s32[2,1]{0,1:T(1,128)S(1)}, bf16[2,512,2048]{2,1,0:T(8,128)(2,1)}, s32[]{:T(128)}) while((s32[]{:T(128)}, bf16[512,2,2048]{2,0,1:T(8,128)(2,1)}, s32[2,1]{0,1:T(1,128)S(1)}, bf16[2,512,2048]{2,1,0:T(8,128)(2,1)}, s32[]{:T(128)}) %tuple.212), condition=%wide.while_cond.8, body=%wide.while_body.8.sunk | while | flops 2 | bytes 4195401 | solution.py:59
  432.5 8.7 %while.21 = (s32[]{:T(128)}, bf16[512,2,2048]{2,0,1:T(8,128)(2,1)}, s32[2,1]{0,1:T(1,128)S(1)}, bf16[2,512,2048]{2,1,0:T(8,128)(2,1)}, s32[]{:T(128)}) while((s32[]{:T(128)}, bf16[512,2,2048]{2,0,1:T(8,128)(2,1)}, s32[2,1]{0,1:T(1,128)S(1)}, bf16[2,512,2048]{2,1,0:T(8,128)(2,1)}, s32[]{:T(128)}) %tuple.213), condition=%wide.while_cond.9, body=%wide.while_body.9.sunk | while | flops 2 | bytes 4195401 | solution.py:59
  443.9 8.9 %while.22 = (s32[]{:T(128)}, bf16[512,2,2048]{2,0,1:T(8,128)(2,1)}, s32[2,1]{0,1:T(1,128)S(1)}, bf16[2,512,2048]{2,1,0:T(8,128)(2,1)}, s32[]{:T(128)}) while((s32[]{:T(128)}, bf16[512,2,2048]{2,0,1:T(8,128)(2,1)}, s32[2,1]{0,1:T(1,128)S(1)}, bf16[2,512,2048]{2,1,0:T(8,128)(2,1)}, s32[]{:T(128)}) %tuple.214), condition=%wide.while_cond.10, body=%wide.while_body.10.sunk | while | flops 2 | bytes 4195401 | solution.py:59
  455.3 9.4 %while.23 = (s32[]{:T(128)}, bf16[512,2,2048]{2,0,1:T(8,128)(2,1)}, s32[2,1]{0,1:T(1,128)S(1)}, bf16[2,512,2048]{2,1,0:T(8,128)(2,1)}, s32[]{:T(128)}) while((s32[]{:T(128)}, bf16[512,2,2048]{2,0,1:T(8,128)(2,1)}, s32[2,1]{0,1:T(1,128)S(1)}, bf16[2,512,2048]{2,1,0:T(8,128)(2,1)}, s32[]{:T(128)}) %tuple.215), condition=%wide.while_cond.11, body=%wide.while_body.11.sunk | while | flops 2 | bytes 4195401 | solution.py:59
  460.6 4.2 bitcast_dynamic-update-slice_fusion.47
  464.7 5.3 bitcast_dynamic-update-slice_fusion.23
  510.1 25.9 %fusion.1 = f32[2,6144,128]{1,2,0:T(8,128)} fusion(bf16[2,128,2048]{2,1,0:T(8,128)(2,1)S(1)} %bitcast.149, bf16[6144,2,2048]{2,0,1:T(8,128)(2,1)} %bitcast_dynamic-update-slice_fusion.12, pred[2]{0:T(512)(128)(4,1)S(1)} %maximum_compare_fusion), kind=kOutput, calls=%fused_computation.33 | convolution fusion | flops 6467616768 | bytes 57671680 | tf_op jit(solution)/shard_map/bri,dbi->brd/dot_general | solution.py:60
  536.0 10.6 %gather_fusion = f32[256,6144]{1,0:T(8,128)} fusion(f32[256,6144]{1,0:T(8,128)} %bitcast.147, s32[1024]{0:T(1024)S(1)} %copy-done.14), kind=kCustom, calls=%fused_computation | custom fusion | bytes 12583936 | tf_op jit(solution)/shard_map/gather | solution.py:66
  546.6 8.4 %reshape.505 = f32[128,2,6144]{2,1,0:T(2,128)} reshape(f32[256,6144]{1,0:T(8,128)} %gather_fusion) | data formatting | bytes 12582912 | tf_op jit(solution)/shard_map/gather | solution.py:66
  555.0 20.2 %fusion = f32[2,128,2048]{2,1,0:T(8,128)} fusion(bf16[6144,2,2048]{2,0,1:T(8,128)(2,1)} %bitcast_dynamic-update-slice_fusion.12, pred[2]{0:T(512)(128)(4,1)S(1)} %maximum_compare_fusion, bf16[2,128,6144]{2,1,0:T(8,128)(2,1)S(1)} %bitcast.148, pred[2,128]{1,0:T(4,128)(4,1)S(1)} %copy-done.22), kind=kOutput, calls=%fused_computation.32 | convolution fusion | flops 6469189632 | bytes 55574784 | tf_op jit(solution)/shard_map/brd,dbi->bri/dot_general | solution.py:63
  581.0 11.9 %multiply_reduce_fusion = bf16[128,6144]{1,0:T(8,128)(2,1)} fusion(f32[128,2,6144]{2,1,0:T(2,128)} %reshape.505, f32[128,2]{1,0:T(8,128)S(1)} %copy.20), kind=kLoop, calls=%fused_computation.35 | loop fusion | flops 2359296 | bytes 7865344 | tf_op jit(solution)/shard_map/reduce_sum | solution.py:66
  592.9 12.6 %copy.30 = bf16[768,2,2048]{2,1,0:T(2,128)(2,1)} copy(bf16[768,2,2048]{2,0,1:T(8,128)(2,1)} %reduce-scatter.5.cloned.1.call-done) | data formatting | bytes 12582912
  605.5 12.9 %psum.7 = f32[128,2]{0,1:T(2,128)} all-reduce(f32[128,2]{0,1:T(2,128)S(1)} %get-tuple-element.225), channel_id=1, replica_groups=mesh['fsdp'=8,'ep'=4] {'ep'}, use_global_device_ids=true, to_apply=%region_14.15 | all-reduce | flops 256 | bytes 2048 | tf_op jit(solution)/shard_map/psum | solution.py:82
  618.5 10.2 %reduce-scatter.3.cloned.1.call-done = bf16[128,1536]{1,0:T(8,128)(2,1)} async-done(((bf16[128,6144]{1,0:T(8,128)(2,1)}), bf16[128,1536]{1,0:T(8,128)(2,1)}) %reduce-scatter.3.cloned.1.call-update) | async-done | bytes 393232 | tf_op jit(solution)/shard_map/reduce_scatter | solution.py:77
  (162 shorter events, 174.6 us)
Async XLA Ops:
  7.2 42.2 %all-gather.5.cloned.1.call-start = ((), (), s32[]{:S(2)}) async-start(), calls=%async_computation.4 | async-start | bytes 1966080 | tf_op jit(solution)/shard_map/all_gather | solution.py:46
  7.9 274.8 %all-gather.3.cloned.1.call-start = ((), (), s32[]{:S(2)}) async-start(), calls=%async_computation.2 | async-start | bytes 56623104 | tf_op jit(solution)/shard_map/all_gather | solution.py:57
  16.3 0.7 copy-start.21
  16.3 4.7 copy-start.19
  16.4 576.5 %reduce-scatter.5.cloned.1.call-start = ((), (), s32[]{:S(2)}) async-start(), calls=%async_computation.5 | async-start | bytes 56623104 | tf_op jit(solution)/shard_map/reduce_scatter | solution.py:69
  17.1 6.4 %copy-start.17 = (s32[128,2]{0,1:T(2,128)}, s32[128,2]{0,1:T(2,128)S(1)}, u32[]{:S(2)}) copy-start(s32[128,2]{0,1:T(2,128)S(1)} %get-tuple-element.112) | copy-start | bytes 3076
  23.2 33.3 %copy-start.15 = (f32[256]{0:T(256)}, f32[256]{0:T(256)S(1)}, u32[]{:S(2)}) copy-start(f32[256]{0:T(256)S(1)} %scatter_custom_fusion) | copy-start | bytes 3076
  56.5 25.0 %copy-start.11 = (bf16[256,6144]{1,0:T(8,128)(2,1)}, bf16[256,6144]{1,0:T(8,128)(2,1)S(1)}, u32[]{:S(2)}) copy-start(bf16[256,6144]{1,0:T(8,128)(2,1)S(1)} %gather_fusion.1) | copy-start | bytes 9437188
  81.5 547.2 %reduce-scatter.3.cloned.1.call-start = ((), (), s32[]{:S(2)}) async-start(), calls=%async_computation.3 | async-start | bytes 1966080 | tf_op jit(solution)/shard_map/reduce_scatter | solution.py:77
  464.7 5.3 copy-start.1
  470.0 3.8 copy-start.2
  473.9 3.9 copy-start.3
  477.7 3.9 copy-start.4
  481.6 3.7 copy-start.5
  485.3 3.7 copy-start.6
  489.0 3.7 copy-start.7
  492.8 3.7 copy-start.8
  496.5 3.7 copy-start.9
  500.2 4.0 copy-start.10
  504.2 3.7 copy-start
  507.9 2.2 copy-start.13
  510.1 25.9 %copy-start.14 = (s32[1024]{0:T(1024)S(1)}, s32[1024]{0:T(1024)}, u32[]{:S(2)}) copy-start(s32[1024]{0:T(1024)} %pad_clamp_fusion.1) | copy-start | bytes 12292
  546.6 8.4 %copy-start.12 = (bf16[256,6144]{1,0:T(8,128)(2,1)S(1)}, bf16[256,6144]{1,0:T(8,128)(2,1)}, u32[]{:S(2)}) copy-start(bf16[256,6144]{1,0:T(8,128)(2,1)} %copy-done.11) | copy-start | bytes 9437188
  546.6 8.4 %copy-start.22 = (pred[2,128]{1,0:T(4,128)(4,1)S(1)}, pred[2,128]{1,0:T(4,128)(4,1)}, u32[]{:S(2)}) copy-start(pred[2,128]{1,0:T(4,128)(4,1)} %fusion.30) | copy-start | bytes 772
  555.0 20.2 %copy-start.16 = (f32[256]{0:T(256)S(1)}, f32[256]{0:T(256)}, u32[]{:S(2)}) copy-start(f32[256]{0:T(256)} %copy-done.15) | copy-start | bytes 3076
  578.4 2.4 copy-start.18
  578.4 2.4 copy-start.20
Sparse Core Ops, SparseCore 0:
  9.6 39.7 all-gather.4
  51.9 230.7 all-gather.2
  286.3 285.8 reduce-scatter.4
  593.0 35.6 reduce-scatter.2
where the time goes:
time: 642 us; the launch traced here: 635 us
  local copies, waits for them, and re-layouts  283 us (44%)
  waiting for transfers between devices  236 us (37%)
  matrix products  71.1 us (11%)
  other arithmetic  17 us (3%)
  between operations  14.3 us (2%)
  blocking collectives  12.9 us (2%)
    all_gather x1, waiting for transfers between devices, local(): piece = lax.all_gather(w_down, 'fsdp', axis=0, tiled=True)  200 us
    gather x48, local copies, waits for them, and re-layouts  109 us
    unnamed x73, local copies, waits for them, and re-layouts  98.7 us
    gather x1, local copies, waits for them, and re-layouts, local(): chosen = jnp.take(piece, safe_exp, axis=1)  41.5 us
    dot_general x1, matrix products, local(): jnp.einsum('bri,dbi->brd', hid_blocks, chosen, preferred_element_type=jnp...  25.9 us
    all_gather x1, waiting for transfers between devices, local(): full_grads = lax.all_gather(grad_out, 'ep', axis=1, tiled=True)  25.9 us
    dot_general x1, matrix products, local(): jnp.einsum('rd,rei->dei', scaled, masked_hid, preferred_element_type=jnp....  24.9 us
    dot_general x1, matrix products, local(): jnp.einsum('brd,dbi->bri', routed_blocks, chosen, preferred_element_type=...  20.2 us
  transfers between devices with their start and end apart: 4, of which 3 were waited for; matrix products, arithmetic and copies ran while one was open for 56% of the time, Pallas kernels for 0%

commit v1 on v0

--- a/solution.py
+++ b/solution.py
@@ -2,8 +2,37 @@
 import jax.numpy as jnp
 from jax import lax
 from jax.sharding import PartitionSpec as P
+from jax.lax import axis_index, axis_size, ppermute
 
 BLOCK = 128
+
+
+def fix_the_cubes(z, d0):
+    all_rows = list(z.shape[1:])
+    all_rows[d0] *= z.shape[0]
+    answer = jnp.moveaxis(z, 0, d0).reshape(all_rows)
+    return answer
+
+
+def reach_blocks(here_x, along_axis):
+    n_axis = axis_size(along_axis)
+    current_arr = here_x[None]
+    for no in range(n_axis.bit_length() - 1):
+        main = 1 << no
+        taken_in = ppermute(
+            current_arr, axis_name=along_axis, perm=[(ix, ix ^ main) for ix in range(n_axis)]
+        )
+        x_now = jnp.stack([current_arr, taken_in])
+        x_new = axis_index(along_axis)
+        base_arr = x_new >> no & 1
+        current_arr = jnp.where(base_arr == 0, x_now, x_now[::-1]).reshape(-1, *here_x.shape)
+    return current_arr
+
+
+def group_islands(arr_in, own_rows, which_dim):
+    f_now = reach_blocks(arr_in, own_rows)
+    next_value = fix_the_cubes(f_now, which_dim)
+    return next_value
 
 
 def route_layout(route_part, prob_part, expert_count, block_rows, row_count):
@@ -43,7 +72,7 @@
     )
     safe_exp = jnp.maximum(block_exp, 0)
     prob_valid = probs * valid.astype(jnp.float32)
-    full_grads = lax.all_gather(grad_out, "ep", axis=1, tiled=True)
+    full_grads = group_islands(grad_out, "ep", 1)
     model_width = full_grads.shape[1]
     routed = jnp.where(row_live[:, None] > 0, full_grads[row_tok], jnp.zeros((), jnp.bfloat16))
     scaled = (row_prob[:, None] * routed.astype(jnp.float32)).astype(jnp.bfloat16)

time: 642 us -> 613 us (0.955)
  waiting for transfers between devices: 236 us -> 202 us
    all_gather x1, waiting for transfers between devices: 200 us -> 156 us  [local(): piece = lax.all_gather(w_down, 'fsdp', axis=0, tiled=True)]
    ppermute x0 -> x2, waiting for transfers between devices: none -> 35.5 us  [reach_blocks(): ppermute(current_arr, axis_name=along_axis, perm=[(ix, ix ^ main) for ix...]
    all_gather x1 -> x0, waiting for transfers between devices: 25.9 us -> none  [local(): full_grads = lax.all_gather(grad_out, 'ep', axis=1, tiled=True)]
    unnamed x73 -> x74, local copies, waits for them, and re-layouts: 98.7 us -> 101 us
  transfers between devices with their start and end apart: 4 -> 5, of which waited for: 3 -> 4; matrix products, arithmetic and copies ran while one was open for 56% -> 57% of each run, Pallas kernels for 0% -> 0%
where the time goes in v1:
time: 613 us; the launch traced here: 605 us
  local copies, waits for them, and re-layouts  283 us (46%)
  waiting for transfers between devices  202 us (33%)
  matrix products  69.5 us (11%)
  other arithmetic  17.1 us (3%)
  between operations  14.3 us (2%)
  blocking collectives  12.8 us (2%)
  starting transfers between devices  6.14 us (1%)
    all_gather x1, waiting for transfers between devices, local(): piece = lax.all_gather(w_down, 'fsdp', axis=0, tiled=True)  156 us
    gather x48, local copies, waits for them, and re-layouts  109 us
    unnamed x74, local copies, waits for them, and re-layouts  101 us
    gather x1, local copies, waits for them, and re-layouts, local(): chosen = jnp.take(piece, safe_exp, axis=1)  41.5 us
    ppermute x2, waiting for transfers between devices, reach_blocks(): ppermute(current_arr, axis_name=along_axis, perm=[(ix, ix ^ main) for ix...  35.5 us
    dot_general x1, matrix products, local(): jnp.einsum('bri,dbi->brd', hid_blocks, chosen, preferred_element_type=jnp...  25.5 us
    dot_general x1, matrix products, local(): jnp.einsum('rd,rei->dei', scaled, masked_hid, preferred_element_type=jnp....  22.6 us
    dot_general x1, matrix products, local(): jnp.einsum('brd,dbi->bri', routed_blocks, chosen, preferred_element_type=...  21.3 us
  transfers between devices with their start and end apart: 5, of which 4 were waited for; matrix products, arithmetic and copies ran while one was open for 57% of the time, Pallas kernels for 0%

profile of v1, /device:TPU:0, one launch (start us, length us, event | category | flops | bytes accessed | tf_op | source)
XLA Modules:
  0.0 605.4 jit_solution(18287039363259036152)
XLA Ops:
  7.2 8.4 %copy.23 = bf16[768,2,2048]{2,0,1:T(8,128)(2,1)} copy(bf16[768,2,2048]{2,1,0:T(2,128)(2,1)} %param.6) | data formatting | bytes 12582912 | tf_op args[1]
  22.4 6.3 %collective-permute-done = bf16[1,128,1536]{2,1,0:T(8,128)(2,1)S(1)} collective-permute-done((bf16[1,128,1536]{2,1,0:T(8,128)(2,1)S(1)}, bf16[1,128,1536]{2,1,0:T(8,128)(2,1)S(1)}, u32[]{:S(2)}, u32[]{:S(2)}) %collective-permute-start) | collective-permute-done | bytes 393248 | tf_op jit(solution)/shard_map/ppermute | solution.py:22
  36.4 29.2 %collective-permute-done.1 = bf16[2,128,1536]{2,1,0:T(8,128)(2,1)S(1)} collective-permute-done((bf16[2,128,1536]{2,1,0:T(8,128)(2,1)S(1)}, bf16[2,128,1536]{2,1,0:T(8,128)(2,1)S(1)}, u32[]{:S(2)}, u32[]{:S(2)}) %collective-permute-start.1) | collective-permute-done | bytes 786464 | tf_op jit(solution)/shard_map/ppermute | solution.py:22
  67.5 4.2 gather_fusion.1
  71.7 22.6 %convolution_convert_fusion = bf16[6144,2,2048]{2,0,1:T(8,128)(2,1)} fusion(bf16[256,6144]{1,0:T(8,128)(2,1)} %gather_fusion.1, f32[256]{0:T(256)S(1)} %scatter_custom_fusion, pred[256]{0:T(512)(128)(4,1)S(1)} %broadcast_compare_fusion, bf16[256,2]{0,1:T(2,128)(2,1)S(1)} %compare_convert_fusion, bf16[256,2048]{1,0:T(8,128)(2,1)S(1)} %copy-done.12), kind=kOutput, calls=%fused_computation.31 | convolution fusion | flops 12920553472 | bytes 54528256 | tf_op jit(solution)/shard_map/rd,rei->dei/dot_general | solution.py:99
  94.5 155.8 %all-gather.2.cloned.1.call-done = bf16[6144,2,2048]{2,0,1:T(8,128)(2,1)} async-done(((bf16[768,2,2048]{2,0,1:T(8,128)(2,1)}), bf16[6144,2,2048]{2,0,1:T(8,128)(2,1)}) %all-gather.2.cloned.1.call-update) | async-done | bytes 50331664 | tf_op jit(solution)/shard_map/all_gather | solution.py:86
  250.3 41.5 %fusion.30 = (bf16[512,2,2048]{2,0,1:T(8,128)(2,1)}, bf16[512,2,2048]{2,0,1:T(8,128)(2,1)}, bf16[512,2,2048]{2,0,1:T(8,128)(2,1)}, bf16[512,2,2048]{2,0,1:T(8,12...) fusion(bf16[6144,2,2048]{2,0,1:T(8,128)(2,1)} %all-gather.2.clo, ...), kind=kLoop, calls=%fused_computation.114 | loop fusion | bytes 100663296 | tf_op jit(solution)/shard_map/jit(_take)/gather | solution.py:88
  294.9 9.6 %while.12 = (s32[]{:T(128)}, bf16[512,2,2048]{2,0,1:T(8,128)(2,1)}, s32[2,1]{0,1:T(1,128)S(1)}, bf16[2,512,2048]{2,1,0:T(8,128)(2,1)}, s32[]{:T(128)}) while((s32[]{:T(128)}, bf16[512,2,2048]{2,0,1:T(8,128)(2,1)}, s32[2,1]{0,1:T(1,128)S(1)}, bf16[2,512,2048]{2,1,0:T(8,128)(2,1)}, s32[]{:T(128)}) %tuple.163), condition=%wide.while_cond, body=%wide.while_body.sunk | while | flops 2 | bytes 4195401 | solution.py:88
  295.5 4.2 bitcast_dynamic-update-slice_fusion.36
  300.3 4.2 bitcast_dynamic-update-slice_fusion.36
  307.6 9.4 %while.13 = (s32[]{:T(128)}, bf16[512,2,2048]{2,0,1:T(8,128)(2,1)}, s32[2,1]{0,1:T(1,128)S(1)}, bf16[2,512,2048]{2,1,0:T(8,128)(2,1)}, s32[]{:T(128)}) while((s32[]{:T(128)}, bf16[512,2,2048]{2,0,1:T(8,128)(2,1)}, s32[2,1]{0,1:T(1,128)S(1)}, bf16[2,512,2048]{2,1,0:T(8,128)(2,1)}, s32[]{:T(128)}) %tuple.205), condition=%wide.while_cond.1, body=%wide.while_body.1.sunk | while | flops 2 | bytes 4195401 | solution.py:88
  308.2 4.3 bitcast_dynamic-update-slice_fusion.37
  319.6 8.9 %while.14 = (s32[]{:T(128)}, bf16[512,2,2048]{2,0,1:T(8,128)(2,1)}, s32[2,1]{0,1:T(1,128)S(1)}, bf16[2,512,2048]{2,1,0:T(8,128)(2,1)}, s32[]{:T(128)}) while((s32[]{:T(128)}, bf16[512,2,2048]{2,0,1:T(8,128)(2,1)}, s32[2,1]{0,1:T(1,128)S(1)}, bf16[2,512,2048]{2,1,0:T(8,128)(2,1)}, s32[]{:T(128)}) %tuple.206), condition=%wide.while_cond.2, body=%wide.while_body.2.sunk | while | flops 2 | bytes 4195401 | solution.py:88
  331.0 9.2 %while.15 = (s32[]{:T(128)}, bf16[512,2,2048]{2,0,1:T(8,128)(2,1)}, s32[2,1]{0,1:T(1,128)S(1)}, bf16[2,512,2048]{2,1,0:T(8,128)(2,1)}, s32[]{:T(128)}) while((s32[]{:T(128)}, bf16[512,2,2048]{2,0,1:T(8,128)(2,1)}, s32[2,1]{0,1:T(1,128)S(1)}, bf16[2,512,2048]{2,1,0:T(8,128)(2,1)}, s32[]{:T(128)}) %tuple.207), condition=%wide.while_cond.3, body=%wide.while_body.3.sunk | while | flops 2 | bytes 4195401 | solution.py:88
  342.8 9.1 %while.16 = (s32[]{:T(128)}, bf16[512,2,2048]{2,0,1:T(8,128)(2,1)}, s32[2,1]{0,1:T(1,128)S(1)}, bf16[2,512,2048]{2,1,0:T(8,128)(2,1)}, s32[]{:T(128)}) while((s32[]{:T(128)}, bf16[512,2,2048]{2,0,1:T(8,128)(2,1)}, s32[2,1]{0,1:T(1,128)S(1)}, bf16[2,512,2048]{2,1,0:T(8,128)(2,1)}, s32[]{:T(128)}) %tuple.208), condition=%wide.while_cond.4, body=%wide.while_body.4.sunk | while | flops 2 | bytes 4195401 | solution.py:88
  354.4 8.8 %while.17 = (s32[]{:T(128)}, bf16[512,2,2048]{2,0,1:T(8,128)(2,1)}, s32[2,1]{0,1:T(1,128)S(1)}, bf16[2,512,2048]{2,1,0:T(8,128)(2,1)}, s32[]{:T(128)}) while((s32[]{:T(128)}, bf16[512,2,2048]{2,0,1:T(8,128)(2,1)}, s32[2,1]{0,1:T(1,128)S(1)}, bf16[2,512,2048]{2,1,0:T(8,128)(2,1)}, s32[]{:T(128)}) %tuple.209), condition=%wide.while_cond.5, body=%wide.while_body.5.sunk | while | flops 2 | bytes 4195401 | solution.py:88
  365.7 8.8 %while.18 = (s32[]{:T(128)}, bf16[512,2,2048]{2,0,1:T(8,128)(2,1)}, s32[2,1]{0,1:T(1,128)S(1)}, bf16[2,512,2048]{2,1,0:T(8,128)(2,1)}, s32[]{:T(128)}) while((s32[]{:T(128)}, bf16[512,2,2048]{2,0,1:T(8,128)(2,1)}, s32[2,1]{0,1:T(1,128)S(1)}, bf16[2,512,2048]{2,1,0:T(8,128)(2,1)}, s32[]{:T(128)}) %tuple.210), condition=%wide.while_cond.6, body=%wide.while_body.6.sunk | while | flops 2 | bytes 4195401 | solution.py:88
  377.1 9.3 %while.19 = (s32[]{:T(128)}, bf16[512,2,2048]{2,0,1:T(8,128)(2,1)}, s32[2,1]{0,1:T(1,128)S(1)}, bf16[2,512,2048]{2,1,0:T(8,128)(2,1)}, s32[]{:T(128)}) while((s32[]{:T(128)}, bf16[512,2,2048]{2,0,1:T(8,128)(2,1)}, s32[2,1]{0,1:T(1,128)S(1)}, bf16[2,512,2048]{2,1,0:T(8,128)(2,1)}, s32[]{:T(128)}) %tuple.211), condition=%wide.while_cond.7, body=%wide.while_body.7.sunk | while | flops 2 | bytes 4195401 | solution.py:88
  377.7 4.2 bitcast_dynamic-update-slice_fusion.43
  388.9 8.8 %while.20 = (s32[]{:T(128)}, bf16[512,2,2048]{2,0,1:T(8,128)(2,1)}, s32[2,1]{0,1:T(1,128)S(1)}, bf16[2,512,2048]{2,1,0:T(8,128)(2,1)}, s32[]{:T(128)}) while((s32[]{:T(128)}, bf16[512,2,2048]{2,0,1:T(8,128)(2,1)}, s32[2,1]{0,1:T(1,128)S(1)}, bf16[2,512,2048]{2,1,0:T(8,128)(2,1)}, s32[]{:T(128)}) %tuple.212), condition=%wide.while_cond.8, body=%wide.while_body.8.sunk | while | flops 2 | bytes 4195401 | solution.py:88
  400.2 8.7 %while.21 = (s32[]{:T(128)}, bf16[512,2,2048]{2,0,1:T(8,128)(2,1)}, s32[2,1]{0,1:T(1,128)S(1)}, bf16[2,512,2048]{2,1,0:T(8,128)(2,1)}, s32[]{:T(128)}) while((s32[]{:T(128)}, bf16[512,2,2048]{2,0,1:T(8,128)(2,1)}, s32[2,1]{0,1:T(1,128)S(1)}, bf16[2,512,2048]{2,1,0:T(8,128)(2,1)}, s32[]{:T(128)}) %tuple.213), condition=%wide.while_cond.9, body=%wide.while_body.9.sunk | while | flops 2 | bytes 4195401 | solution.py:88
  411.5 9.0 %while.22 = (s32[]{:T(128)}, bf16[512,2,2048]{2,0,1:T(8,128)(2,1)}, s32[2,1]{0,1:T(1,128)S(1)}, bf16[2,512,2048]{2,1,0:T(8,128)(2,1)}, s32[]{:T(128)}) while((s32[]{:T(128)}, bf16[512,2,2048]{2,0,1:T(8,128)(2,1)}, s32[2,1]{0,1:T(1,128)S(1)}, bf16[2,512,2048]{2,1,0:T(8,128)(2,1)}, s32[]{:T(128)}) %tuple.214), condition=%wide.while_cond.10, body=%wide.while_body.10.sunk | while | flops 2 | bytes 4195401 | solution.py:88
  423.0 9.4 %while.23 = (s32[]{:T(128)}, bf16[512,2,2048]{2,0,1:T(8,128)(2,1)}, s32[2,1]{0,1:T(1,128)S(1)}, bf16[2,512,2048]{2,1,0:T(8,128)(2,1)}, s32[]{:T(128)}) while((s32[]{:T(128)}, bf16[512,2,2048]{2,0,1:T(8,128)(2,1)}, s32[2,1]{0,1:T(1,128)S(1)}, bf16[2,512,2048]{2,1,0:T(8,128)(2,1)}, s32[]{:T(128)}) %tuple.215), condition=%wide.while_cond.11, body=%wide.while_body.11.sunk | while | flops 2 | bytes 4195401 | solution.py:88
  432.4 5.3 bitcast_dynamic-update-slice_fusion.23
  479.0 21.3 %fusion = f32[2,128,2048]{2,1,0:T(8,128)} fusion(bf16[6144,2,2048]{2,0,1:T(8,128)(2,1)} %bitcast_dynamic-update-slice_fusion.12, pred[2]{0:T(512)(128)(4,1)S(1)} %maximum_compare_fusion, bf16[2,128,6144]{2,1,0:T(8,128)(2,1)S(1)} %bitcast.161, pred[2,128]{1,0:T(4,128)(4,1)S(1)} %fusion.32), kind=kOutput, calls=%fused_computation.32 | convolution fusion | flops 6469189632 | bytes 55574784 | tf_op jit(solution)/shard_map/brd,dbi->bri/dot_general | solution.py:92
  505.9 25.5 %fusion.1 = f32[2,6144,128]{1,2,0:T(8,128)} fusion(bf16[2,128,2048]{2,1,0:T(8,128)(2,1)S(1)} %bitcast.162, bf16[6144,2,2048]{2,0,1:T(8,128)(2,1)} %bitcast_dynamic-update-slice_fusion.12, pred[2]{0:T(512)(128)(4,1)S(1)} %maximum_compare_fusion), kind=kOutput, calls=%fused_computation.33 | convolution fusion | flops 6467616768 | bytes 57671680 | tf_op jit(solution)/shard_map/bri,dbi->brd/dot_general | solution.py:89
  531.4 10.6 %gather_fusion = f32[256,6144]{1,0:T(8,128)} fusion(f32[256,6144]{1,0:T(8,128)} %bitcast.160, s32[1024]{0:T(1024)S(1)} %copy-done.14), kind=kCustom, calls=%fused_computation | custom fusion | bytes 12583936 | tf_op jit(solution)/shard_map/gather | solution.py:95
  542.0 8.4 %reshape.517 = f32[128,2,6144]{2,1,0:T(2,128)} reshape(f32[256,6144]{1,0:T(8,128)} %gather_fusion) | data formatting | bytes 12582912 | tf_op jit(solution)/shard_map/gather | solution.py:95
  550.4 11.9 %multiply_reduce_fusion = bf16[128,6144]{1,0:T(8,128)(2,1)} fusion(f32[128,2,6144]{2,1,0:T(2,128)} %reshape.517, f32[128,2]{1,0:T(8,128)S(1)} %copy.22), kind=kLoop, calls=%fused_computation.35 | loop fusion | flops 2359296 | bytes 7865344 | tf_op jit(solution)/shard_map/reduce_sum | solution.py:95
  562.3 12.6 %copy.33 = bf16[768,2,2048]{2,1,0:T(2,128)(2,1)} copy(bf16[768,2,2048]{2,0,1:T(8,128)(2,1)} %reduce-scatter.5.cloned.1.call-done) | data formatting | bytes 12582912
  574.9 12.8 %psum.7 = f32[128,2]{0,1:T(2,128)} all-reduce(f32[128,2]{0,1:T(2,128)S(1)} %get-tuple-element.227), channel_id=1, replica_groups=mesh['fsdp'=8,'ep'=4] {'ep'}, use_global_device_ids=true, to_apply=%region_14.15 | all-reduce | flops 256 | bytes 2048 | tf_op jit(solution)/shard_map/psum | solution.py:111
  587.7 10.9 %reduce-scatter.3.cloned.1.call-done = bf16[128,1536]{1,0:T(8,128)(2,1)} async-done(((bf16[128,6144]{1,0:T(8,128)(2,1)}), bf16[128,1536]{1,0:T(8,128)(2,1)}) %reduce-scatter.3.cloned.1.call-update) | async-done | bytes 393232 | tf_op jit(solution)/shard_map/reduce_scatter | solution.py:106
  (168 shorter events, 187.0 us)
Async XLA Ops:
  7.2 243.2 %all-gather.2.cloned.1.call-start = ((), (), s32[]{:S(2)}) async-start(), calls=%async_computation.2 | async-start | bytes 56623104 | tf_op jit(solution)/shard_map/all_gather | solution.py:86
  15.6 1.0 copy-start.15
  15.6 4.0 copy-start.22
  15.6 17.9 %copy-start.20 = (f32[128,2]{0,1:T(2,128)S(1)}, f32[128,2]{0,1:T(2,128)}, u32[]{:S(2)}) copy-start(f32[128,2]{0,1:T(2,128)} %param.8) | copy-start | bytes 3076
  15.6 546.7 %reduce-scatter.5.cloned.1.call-start = ((), (), s32[]{:S(2)}) async-start(), calls=%async_computation.4 | async-start | bytes 56623104 | tf_op jit(solution)/shard_map/reduce_scatter | solution.py:98
  16.6 12.1 %collective-permute-start = (bf16[1,128,1536]{2,1,0:T(8,128)(2,1)S(1)}, bf16[1,128,1536]{2,1,0:T(8,128)(2,1)S(1)}, u32[]{:S(2)}, u32[]{:S(2)}) collective-permute-start(bf16[1,128,1536]{2,1,0:T(8,128)(2,1)S(1)} %bitcast.166), channel_id=1, source_target_pairs={{0,1},{1,0},{2,3},{3,2},{4,5},{5,4},{6,7},{7,6},{8,9},{9,8},{10,11... | collective-permute-start | bytes 1179656 | tf_op jit(solution)/shard_map/ppermute | solution.py:22
  19.7 9.0 %copy-start.18 = (s32[128,2]{0,1:T(2,128)}, s32[128,2]{0,1:T(2,128)S(1)}, u32[]{:S(2)}) copy-start(s32[128,2]{0,1:T(2,128)S(1)} %get-tuple-element.112) | copy-start | bytes 3076
  29.0 36.5 %collective-permute-start.1 = (bf16[2,128,1536]{2,1,0:T(8,128)(2,1)S(1)}, bf16[2,128,1536]{2,1,0:T(8,128)(2,1)S(1)}, u32[]{:S(2)}, u32[]{:S(2)}) collective-permute-start(bf16[2,128,1536]{2,1,0:T(8,128)(2,1)S(1)} %get-tuple-element.226), channel_id=1, source_target_pairs={{0,2},{1,3},{2,0},{3,1},{4,6},{5,7},{6,4},{7,5},{8,10},{9,11},{10,... | collective-permute-start | bytes 2359304 | tf_op jit(solution)/shard_map/ppermute | solution.py:22
  35.7 36.0 %copy-start.16 = (f32[256]{0:T(256)}, f32[256]{0:T(256)S(1)}, u32[]{:S(2)}) copy-start(f32[256]{0:T(256)S(1)} %scatter_custom_fusion) | copy-start | bytes 3076
  67.5 4.2 copy-start.12
  94.3 504.3 %reduce-scatter.3.cloned.1.call-start = ((), (), s32[]{:S(2)}) async-start(), calls=%async_computation.3 | async-start | bytes 1966080 | tf_op jit(solution)/shard_map/reduce_scatter | solution.py:106
  432.4 5.3 copy-start.1
  437.6 3.8 copy-start.2
  441.5 3.9 copy-start.3
  445.4 3.8 copy-start.4
  449.2 3.7 copy-start.5
  452.9 3.7 copy-start.6
  456.6 3.7 copy-start.7
  460.4 3.7 copy-start.8
  464.1 3.7 copy-start.9
  467.8 4.0 copy-start.10
  471.8 3.7 copy-start
  475.5 3.5 copy-start.11
  479.0 21.3 %copy-start.17 = (f32[256]{0:T(256)S(1)}, f32[256]{0:T(256)}, u32[]{:S(2)}) copy-start(f32[256]{0:T(256)} %copy-done.16) | copy-start | bytes 3076
  500.3 3.2 copy-start.14
  503.5 2.2 copy-start.19
  503.5 2.2 copy-start.21
  503.6 2.3 copy-start.13
Sparse Core Ops, SparseCore 0:
  15.7 234.5 all-gather.1
  254.0 285.8 reduce-scatter.4
  562.4 36.1 reduce-scatter.2
